TPU v7x, 256 devices: a whole 4x4x8 slice. The times are simulated.
256 devices in a mesh: tests: 64 (over z, x, core), branches: 4 (over y).
Axes of the slice: x: 4, y: 4, z: 8, core: 2. Of those that a mesh axis runs over, the one named last changes fastest.
Arguments:
- select: float32 [1048576], P('tests'), may hold values from 1e-05 to 0.95
- tiles: float32 [16384, 128, 128], P(('tests', 'branches')), may hold values from 0.0001 to 0.9
- row_block: int32 [16384], P(('tests', 'branches')), may hold values from 0 to 127
- col_block: int32 [16384], P(('tests', 'branches')), may hold values from 0 to 2047, as said below
- counts: int32 [256], P(('tests', 'branches')), may hold values from 1 to 64, 10240 in all
- weights: float32 [1048576], P('branches'), may hold values from 1 to 16
Outputs:
- grad_tests: float32 [1048576], P('tests')
- tile_grads: float32 [16384, 128, 128], P(('tests', 'branches'))
- next_select: float32 [1048576], P('tests')
Inputs may be any that keep to these rules, and one draw needn't show every extreme that they name: counts[d] is the number of device d's slots, from its first, that hold tiles. Call col_block[s] // 32 the share of slot s. Of the 64 slots of one device at most 2 have one share; in every index of branches one share holds exactly 2 slots of every device there.
All inputs are finite; a program needn't handle non-finite values.
Results may differ from a plain program's by a relative error of at most 0.0003.
Values sent between devices are 32-bit elements; how exact they have to be, the bound alone decides.
A program may use at most 64 MiB of HBM per device.

v0:
```python
import jax
import jax.numpy as jnp
from jax import lax
from jax.sharding import PartitionSpec as P

STEPS = 2
ascent_rate = 0.0015
select_cap = 0.5


def tile_logs(blocks, tiles, rows, live):
    picked = blocks[rows]
    logs = jnp.sum(jnp.log1p(-picked[:, :, None] * tiles), axis=1)
    return jnp.where(live[:, None], logs, jnp.zeros_like(logs))


def tile_terms(blocks, slot_survive, tiles, rows, live):
    picked = blocks[rows]
    inverse = 1.0 / (1.0 - picked[:, :, None] * tiles)
    scaled = slot_survive[:, None, :] * inverse
    tests_part = jnp.sum(scaled * tiles, axis=2)
    tests_part = jnp.where(live[:, None], tests_part, jnp.zeros_like(tests_part))
    tile_part = scaled * picked[:, :, None]
    tile_part = jnp.where(live[:, None, None], tile_part, jnp.zeros_like(tile_part))
    return (tests_part, tile_part)


def body(select, tiles, row_block, col_block, counts, weights):
    width = tiles.shape[1]
    slots = tiles.shape[0]
    test_rows = select.shape[0] // width
    branch_rows = weights.shape[0] // width
    weight_rows = weights.reshape(branch_rows, width)
    limit = counts[0]
    current = select
    grad_tests = select
    tile_grads = tiles
    for step in range(STEPS):
        keep = step == STEPS - 1
        blocks = current.reshape(test_rows, width)
        live = jnp.arange(slots, dtype=jnp.int32) < limit
        slot_logs = tile_logs(blocks, tiles, row_block, live)
        partial_value = jnp.zeros((branch_rows, width), jnp.float32).at[col_block].add(slot_logs)
        summed = lax.psum(partial_value, "tests")
        slot_survive = (weight_rows * jnp.exp(summed))[col_block]
        empty_tests = jnp.zeros((test_rows, width), jnp.float32)
        live = jnp.arange(slots, dtype=jnp.int32) < limit
        tests_part, tile_part = tile_terms(blocks, slot_survive, tiles, row_block, live)
        tests_sum = empty_tests.at[row_block].add(tests_part)
        gradient = lax.psum(tests_sum, "branches").reshape(-1)
        if keep:
            grad_tests = gradient
            tile_grads = tile_part
        rate = ascent_rate * gradient
        current = current + (select_cap - current) * rate / (1.0 + rate)
    return (grad_tests, tile_grads, current)


def solution(mesh):
    return jax.shard_map(
        body,
        mesh=mesh,
        in_specs=(
            P("tests"),
            P(("tests", "branches"), None, None),
            P(("tests", "branches")),
            P(("tests", "branches")),
            P(("tests", "branches")),
            P("branches"),
        ),
        out_specs=(P("tests"), P(("tests", "branches"), None, None), P("tests")),
        check_vma=False,
    )
```

profile of v0, /device:TPU:2, one launch (start us, length us, event | category | flops | bytes accessed | tf_op | source)
XLA Modules:
  0.0 514.2 jit_solution(9038397558886190916)
XLA Ops:
  7.2 0.0 all-reduce.5.cloned.1.call-start
  8.0 0.7 compare_select_fusion.1
  8.6 0.7 compare_select_fusion
  9.3 1.4 gather_fusion
  10.7 3.3 log-plus-one_reduce_fusion.1
  14.1 1.9 scatter_custom_fusion
  15.9 0.0 all-reduce.5.cloned.1.call-update
  16.0 0.0 copy-start.1
  16.0 0.0 all-reduce.7.cloned.1.call-start
  16.0 189.7 %all-reduce.5.cloned.1.call-done = f32[2048,128]{1,0:T(8,128)} async-done(((f32[2048,128]{1,0:T(8,128)}), f32[2048,128]{1,0:T(8,128)}) %all-reduce.5.cloned.1.call-update) | async-done | bytes 1048592 | tf_op jit(solution)/shard_map/psum | solution.py:44
  205.7 1.4 bitcast_multiply_fusion.1
  207.1 0.6 gather_fusion.1
  207.7 4.5 multiply_reduce_fusion.1
  212.2 1.5 scatter_custom_fusion.1
  213.7 0.0 all-reduce.7.cloned.1.call-update
  213.7 0.0 all-reduce.9.cloned.1.call-start
  213.8 43.7 %all-reduce.7.cloned.1.call-done = f32[128,128]{1,0:T(8,128)} async-done(((f32[128,128]{1,0:T(8,128)}), f32[128,128]{1,0:T(8,128)}) %all-reduce.7.cloned.1.call-update) | async-done | bytes 65552 | tf_op jit(solution)/shard_map/psum | solution.py:50
  257.4 0.9 fusion.22
  258.3 0.6 gather_fusion.2
  258.9 3.3 log-plus-one_reduce_fusion
  262.2 1.9 scatter_custom_fusion.2
  264.1 0.0 all-reduce.9.cloned.1.call-update
  264.1 0.0 all-reduce.11.cloned.1.call-start
  264.2 187.4 %all-reduce.9.cloned.1.call-done = f32[2048,128]{1,0:T(8,128)} async-done(((f32[2048,128]{1,0:T(8,128)}), f32[2048,128]{1,0:T(8,128)}) %all-reduce.9.cloned.1.call-update) | async-done | bytes 1048592 | tf_op jit(solution)/shard_map/psum | solution.py:44
  451.6 1.4 bitcast_multiply_fusion
  453.0 0.6 gather_fusion.3
  453.6 5.9 %multiply_select_fusion = (f32[64,128,128]{2,1,0:T(8,128)}, f32[64,128]{1,0:T(8,128)S(1)}) fusion(f32[64,128,128]{2,1,0:T(8,128)} %param.7, f32[64,128]{1,0:T(8,128)S(1)} %gather_fusion.2, f32[64,128]{1,0:T(8,128)S(1)} %gather_fusion.3, pred[64]{0:T(512)(128)(4,1)S(1)} %iota_compare_fusion), kind=kLoop, calls=%fused_computation.8 | loop fusion | flops 8380416 | bytes 8486976 | tf_op jit(solution)/shard_map/jit(_where)/select_n | solution.py:24
  459.5 1.5 scatter_custom_fusion.3
  460.9 0.0 all-reduce.11.cloned.1.call-update
  460.9 43.7 %all-reduce.11.cloned.1.call-done = f32[16384]{0:T(1024)} async-done(((f32[16384]{0:T(1024)}), f32[16384]{0:T(1024)}) %all-reduce.11.cloned.1.call-update) | async-done | bytes 65552 | tf_op jit(solution)/shard_map/psum | solution.py:50
  504.7 1.5 divide_add_fusion
  506.2 1.5 copy.14
  (10 shorter events, 0.0 us)
Async XLA Ops:
  7.2 198.6 %copy-start = (f32[262144]{0:T(1024)S(1)}, f32[262144]{0:T(1024)}, u32[]{:S(2)}) copy-start(f32[262144]{0:T(1024)} %param.11) | copy-start | bytes 3145732
  7.2 198.6 %all-reduce.5.cloned.1.call-start = ((), (), s32[]{:S(2)}) async-start(), calls=%async_computation | async-start | bytes 2097152 | tf_op jit(solution)/shard_map/psum | solution.py:44
  16.0 241.5 %copy-start.1 = (f32[16384]{0:T(1024)S(1)}, f32[16384]{0:T(1024)}, u32[]{:S(2)}) copy-start(f32[16384]{0:T(1024)} %param.6) | copy-start | bytes 196612
  16.0 241.4 %all-reduce.7.cloned.1.call-start = ((), (), s32[]{:S(2)}) async-start(), calls=%async_computation.1 | async-start | bytes 131072 | tf_op jit(solution)/shard_map/psum | solution.py:50
  213.7 237.9 %all-reduce.9.cloned.1.call-start = ((), (), s32[]{:S(2)}) async-start(), calls=%async_computation.2 | async-start | bytes 2097152 | tf_op jit(solution)/shard_map/psum | solution.py:44
  264.1 240.5 %all-reduce.11.cloned.1.call-start = ((), (), s32[]{:S(2)}) async-start(), calls=%async_computation.3 | async-start | bytes 131072 | tf_op jit(solution)/shard_map/psum | solution.py:50
  453.6 51.1 %copy-start.2 = (f32[128,128]{1,0:T(8,128)S(1)}, f32[128,128]{1,0:T(8,128)}, u32[]{:S(2)}) copy-start(f32[128,128]{1,0:T(8,128)} %all-reduce.7.cloned.1.call-done) | copy-start | bytes 196612
Sparse Core Ops, SparseCore 0:
  16.1 189.6 all-reduce.4
  213.8 43.5 all-reduce.6
  264.3 187.3 all-reduce.8
  461.1 43.5 all-reduce.10
where the time goes:
time: 515 us; the launch traced here: 514 us
  waiting for transfers between devices  465 us (90%)
  other arithmetic  30.2 us (6%)
  between operations  14.6 us (3%)
    psum x2, waiting for transfers between devices, body(): summed = lax.psum(partial_value, 'tests')  377 us
    psum x2, waiting for transfers between devices, body(): gradient = lax.psum(tests_sum, 'branches').reshape(-1)  87.4 us
  transfers between devices with their start and end apart: 4, of which 4 were waited for; matrix products, arithmetic and copies ran while one was open for 0% of the time, Pallas kernels for 0%

commit v1 on v0

--- a/solution.py
+++ b/solution.py
@@ -47,7 +47,10 @@
         live = jnp.arange(slots, dtype=jnp.int32) < limit
         tests_part, tile_part = tile_terms(blocks, slot_survive, tiles, row_block, live)
         tests_sum = empty_tests.at[row_block].add(tests_part)
-        gradient = lax.psum(tests_sum, "branches").reshape(-1)
+        balance_the_tiles = lambda my_data, along_axis: jnp.sum(
+            jax.lax.all_gather(my_data, along_axis), 0
+        )
+        gradient = balance_the_tiles(tests_sum, "branches").reshape(-1)
         if keep:
             grad_tests = gradient
             tile_grads = tile_part

time: 515 us -> 445 us (0.86)
  waiting for transfers between devices: 465 us -> 373 us
  blocking collectives: 0 us -> 25.7 us
    psum x2 -> x0, waiting for transfers between devices: 87.4 us -> none  [body(): gradient = lax.psum(tests_sum, 'branches').reshape(-1)]
    all_gather x0 -> x2, blocking collectives: none -> 25.7 us  [body(): jax.lax.all_gather(my_data, along_axis)]
  transfers between devices with their start and end apart: 4 -> 2, of which waited for: 4 -> 2; matrix products, arithmetic and copies ran while one was open for 0% -> 0% of each run, Pallas kernels for 0% -> 0%
where the time goes in v1:
time: 445 us; the launch traced here: 444 us
  waiting for transfers between devices  373 us (84%)
  other arithmetic  27.3 us (6%)
  blocking collectives  25.7 us (6%)
  between operations  14.9 us (3%)
    psum x2, waiting for transfers between devices, body(): summed = lax.psum(partial_value, 'tests')  373 us
    all_gather x2, blocking collectives, body(): jax.lax.all_gather(my_data, along_axis)  25.7 us
  transfers between devices with their start and end apart: 2, of which 2 were waited for; matrix products, arithmetic and copies ran while one was open for 0% of the time, Pallas kernels for 0%

profile of v1, /device:TPU:2, one launch (start us, length us, event | category | flops | bytes accessed | tf_op | source)
XLA Modules:
  0.0 444.4 jit_solution(1126891048918274531)
XLA Ops:
  7.2 0.0 copy-start
  7.2 0.0 all-reduce.3.cloned.1.call-start
  8.0 0.7 compare_select_fusion.1
  8.6 0.7 compare_select_fusion
  9.3 1.4 gather_fusion
  10.7 3.3 log-plus-one_reduce_fusion.1
  14.1 1.9 scatter_custom_fusion
  15.9 0.0 all-reduce.3.cloned.1.call-update
  16.0 0.0 all-reduce.5.cloned.1.call-start
  16.0 0.0 copy-start.1
  16.0 189.7 %all-reduce.3.cloned.1.call-done = f32[2048,128]{1,0:T(8,128)} async-done(((f32[2048,128]{1,0:T(8,128)}), f32[2048,128]{1,0:T(8,128)}) %all-reduce.3.cloned.1.call-update) | async-done | bytes 1048592 | tf_op jit(solution)/shard_map/psum | solution.py:44
  205.7 0.0 copy-done
  205.7 1.4 bitcast_multiply_fusion.1
  207.1 0.6 gather_fusion.1
  207.7 4.5 %multiply_reduce_fusion.1 = f32[64,128]{1,0:T(8,128)S(1)} fusion(f32[64,128,128]{2,1,0:T(8,128)} %param.7, f32[64,128]{1,0:T(8,128)S(1)} %gather_fusion, f32[64,128]{1,0:T(8,128)S(1)} %gather_fusion.1), kind=kLoop, calls=%fused_computation.12 | loop fusion | flops 6283264 | bytes 4292608 | tf_op jit(solution)/shard_map/reduce_sum | solution.py:21
  212.2 0.9 scatter_custom_fusion.1
  213.1 12.9 %all-gather = f32[512,128]{1,0:T(8,128)S(1)} all-gather(f32[128,128]{1,0:T(8,128)S(1)} %scatter_custom_fusion.1), channel_id=2, replica_groups=mesh['tests'=64,'branches'=4] {'branches'}, dimensions={0}, use_global_device_ids=true | all-gather | bytes 327680 | tf_op jit(solution)/shard_map/all_gather | solution.py:51
  226.0 0.0 copy-done.1
  226.1 0.6 gather_fusion.2
  226.7 3.3 log-plus-one_reduce_fusion
  230.0 1.9 scatter_custom_fusion.2
  231.9 0.0 all-reduce.5.cloned.1.call-update
  231.9 183.4 %all-reduce.5.cloned.1.call-done = f32[2048,128]{1,0:T(8,128)} async-done(((f32[2048,128]{1,0:T(8,128)}), f32[2048,128]{1,0:T(8,128)}) %all-reduce.5.cloned.1.call-update) | async-done | bytes 1048592 | tf_op jit(solution)/shard_map/psum | solution.py:44
  415.3 1.4 bitcast_multiply_fusion
  416.6 0.6 gather_fusion.3
  417.2 5.8 %multiply_select_fusion = (f32[64,128,128]{2,1,0:T(8,128)}, f32[64,128]{1,0:T(8,128)S(1)}) fusion(f32[64,128,128]{2,1,0:T(8,128)} %param.7, f32[64,128]{1,0:T(8,128)S(1)} %gather_fusion.2, f32[64,128]{1,0:T(8,128)S(1)} %gather_fusion.3, pred[64]{0:T(512)(128)(4,1)S(1)} %iota_compare_fusion), kind=kLoop, calls=%fused_computation.8 | loop fusion | flops 8380416 | bytes 8486976 | tf_op jit(solution)/shard_map/jit(_where)/select_n | solution.py:24
  423.1 0.9 scatter_custom_fusion.3
  424.0 12.9 %all-gather.1 = f32[512,128]{1,0:T(8,128)S(1)} all-gather(f32[128,128]{1,0:T(8,128)S(1)} %scatter_custom_fusion.3), channel_id=3, replica_groups=mesh['tests'=64,'branches'=4] {'branches'}, dimensions={0}, use_global_device_ids=true | all-gather | bytes 327680 | tf_op jit(solution)/shard_map/all_gather | solution.py:51
  436.9 0.0 copy-start.2
  436.9 0.7 divide_add_fusion
  437.6 0.0 copy-done.2
  (8 shorter events, 0.1 us)
Async XLA Ops:
  7.2 198.6 %copy-start = (f32[262144]{0:T(1024)S(1)}, f32[262144]{0:T(1024)}, u32[]{:S(2)}) copy-start(f32[262144]{0:T(1024)} %param.11) | copy-start | bytes 3145732
  7.2 198.6 %all-reduce.3.cloned.1.call-start = ((), (), s32[]{:S(2)}) async-start(), calls=%async_computation | async-start | bytes 2097152 | tf_op jit(solution)/shard_map/psum | solution.py:44
  16.0 399.3 %all-reduce.5.cloned.1.call-start = ((), (), s32[]{:S(2)}) async-start(), calls=%async_computation.1 | async-start | bytes 2097152 | tf_op jit(solution)/shard_map/psum | solution.py:44
  16.0 210.0 %copy-start.1 = (f32[16384]{0:T(1024)S(1)}, f32[16384]{0:T(1024)}, u32[]{:S(2)}) copy-start(f32[16384]{0:T(1024)} %param.6) | copy-start | bytes 196612
  436.9 0.7 copy-start.2
Sparse Core Ops, SparseCore 0:
  16.1 189.6 all-reduce.2
  232.0 183.2 all-reduce.4
